TPU v7x, 32 devices: a whole 2x2x4 slice. The times are simulated.
32 devices in a mesh: bin: 8 (over z, y), sky: 4 (over x, core).
Axes of the slice: x: 2, y: 2, z: 4, core: 2. Of those that a mesh axis runs over, the one named last changes fastest.
Arguments:
- lensing_maps: bfloat16 [8, 32, 8192], P('bin', 'sky')
- filter_taps: float32 [5, 17], replicated, may hold values from -1.5 to 1.5
- survey_mask: int32 [4, 64], P('sky'), may hold values 0 or 1
- bin_pairs: int32 [36, 2], replicated, may hold values from 0 to 7, as said below
- target_corr: float32 [36, 5, 4], replicated, may hold values from -3 to 3
- pair_weight: float32 [36, 5, 4], replicated, may hold values from 0.3 to 3
Outputs:
- corr_table: float32 [36, 5, 4], replicated
- map_gradient: float32 [8, 32, 8192], P('bin', 'sky')
Inputs may be any that keep to these rules, and one draw needn't show every extreme that they name: `bin_pairs`: every unordered pair of the 8 bins, a bin with itself included, is listed exactly once; the order of the list and of the two bins in a row vary.
All inputs are finite; a program needn't handle non-finite values. No bound on the sum of `survey_mask` on one device may be relied on, other than what follows from the above.
Results may differ from a plain program's by a relative error of at most 0.0015.
Values may be sent and summed in bfloat16 or wider, within the bound.
A program may use at most 64 MiB of HBM per device.

v0:
```python
import jax
import jax.numpy as jnp
from jax import lax
from jax.sharding import PartitionSpec as P

HIGH = lax.Precision.HIGHEST


def with_halo(block, sides, width):
    for axis, dim in sides:
        count = lax.axis_size(axis)
        forward = [(i, i + 1) for i in range(count - 1)]
        backward = [(target, source) for source, target in forward]
        low = lax.ppermute(
            lax.slice_in_dim(block, block.shape[dim] - width, None, axis=dim), axis, forward
        )
        high = lax.ppermute(lax.slice_in_dim(block, 0, width, axis=dim), axis, backward)
        block = jnp.concatenate([low, block, high], axis=dim)
    return block


def shifted(value, axis, steps):
    count = lax.axis_size(axis)
    pairs = [(source, (source + steps) % count) for source in range(count)]
    return lax.ppermute(value, axis, pairs)


def expand_mask(survey_mask):
    values = survey_mask.astype(jnp.float32)
    tiles_x, tiles_y = values.shape
    return jnp.broadcast_to(values[:, None, :, None], (tiles_x, 8, tiles_y, 128)).reshape(
        tiles_x * 8, tiles_y * 128
    )


def smooth(haloed, filter_taps, row_count):
    tap_count = filter_taps.shape[1]
    half_width = (tap_count - 1) // 2
    widened = haloed.astype(jnp.float32)
    across = filter_taps[:, 0, None, None] * widened[None, 0:row_count]
    for a in range(1, tap_count):
        across = across + filter_taps[:, a, None, None] * widened[None, a : a + row_count]
    padded = jnp.pad(across, ((0, 0), (0, 0), (half_width, half_width)))
    col_count = widened.shape[1]
    result = filter_taps[:, 0, None, None] * padded[:, :, 0:col_count]
    for c in range(1, tap_count):
        result = result + filter_taps[:, c, None, None] * padded[:, :, c : c + col_count]
    return result.astype(jnp.bfloat16)


def lagged(left_maps, right_maps, pixmask, lag_count):
    col_count = left_maps.shape[2]
    columns = []
    for offset in range(lag_count):
        joint_mask = pixmask[:, : col_count - offset] * pixmask[:, offset:]
        product = (
            left_maps[:, :, : col_count - offset].astype(jnp.float32)
            * right_maps[:, :, offset:].astype(jnp.float32)
            * joint_mask[None]
        )
        columns.append(jnp.sum(product, axis=(1, 2)))
    return jnp.stack(columns, axis=1)


def adjoint_lags(partner, ahead_w, behind_w, pixmask):
    col_count = partner.shape[2]
    widened = partner.astype(jnp.float32)
    totals = jnp.zeros(partner.shape, jnp.float32)
    for offset in range(ahead_w.shape[1]):
        joint_mask = pixmask[:, : col_count - offset] * pixmask[:, offset:]
        front = jnp.pad(joint_mask[None] * widened[:, :, offset:], ((0, 0), (0, 0), (0, offset)))
        back = jnp.pad(
            joint_mask[None] * widened[:, :, : col_count - offset], ((0, 0), (0, 0), (offset, 0))
        )
        totals = (
            totals + ahead_w[:, offset, None, None] * front + behind_w[:, offset, None, None] * back
        )
    return totals


def adjoint_cols(grads, filter_taps):
    tap_count = filter_taps.shape[1]
    half_width = (tap_count - 1) // 2
    col_count = grads.shape[2]
    padded = jnp.pad(grads, ((0, 0), (0, 0), (half_width, half_width)))
    result = filter_taps[:, tap_count - 1, None, None] * padded[:, :, 0:col_count]
    for c in range(1, tap_count):
        result = (
            result + filter_taps[:, tap_count - 1 - c, None, None] * padded[:, :, c : c + col_count]
        )
    return result


def adjoint_rows(widened, filter_taps, row_count):
    tap_count = filter_taps.shape[1]
    result = filter_taps[:, tap_count - 1, None, None] * widened[:, 0:row_count]
    for a in range(1, tap_count):
        result = (
            result + filter_taps[:, tap_count - 1 - a, None, None] * widened[:, a : a + row_count]
        )
    return jnp.sum(result, axis=0)


def put_block(row_hot, col_hot, values):
    return row_hot[:, None, None, None] * col_hot[None, :, None, None] * values[None, None]


def take_block(table, row_hot, col_hot):
    return jnp.einsum("i,j,ijsl->sl", row_hot, col_hot, table, precision=HIGH)


def per_device(lensing_maps, filter_taps, survey_mask, bin_pairs, target_corr, pair_weight):
    tap_count = filter_taps.shape[1]
    half_width = (tap_count - 1) // 2
    my_strip = lensing_maps[0]
    row_count, col_count = my_strip.shape
    bin_count = lax.axis_size("bin")
    sky_count = lax.axis_size("sky")
    my_bin = lax.axis_index("bin")
    lag_count = pair_weight.shape[2]
    inverse_area = 1.0 / (row_count * sky_count * col_count)
    pixmask = expand_mask(survey_mask)
    haloed = with_halo(my_strip, (("sky", 0),), half_width)
    own_maps = smooth(haloed, filter_taps, row_count)

    def forward_move(carried):
        moved = shifted(carried, "bin", 1)
        return moved

    indices = jnp.arange(bin_count, dtype=jnp.int32)
    mine_hot = (indices == my_bin).astype(jnp.float32)

    def bin_hot(k):
        return (indices == (my_bin - k) % bin_count).astype(jnp.float32)

    visit_count = bin_count - 1
    stored_init = jnp.zeros((visit_count,) + own_maps.shape, own_maps.dtype)

    def keep_visitor(stored, carried, k):
        stored = lax.dynamic_update_index_in_dim(stored, carried, k - 1, 0)
        return stored

    initial = put_block(
        mine_hot, mine_hot, lagged(own_maps, own_maps, pixmask, lag_count) * inverse_area
    )

    def advance(k, state_all):
        carried, tables, stored = state_all
        carried = forward_move(carried)
        stored = keep_visitor(stored, carried, k)
        tables = tables + put_block(
            mine_hot, bin_hot(k), lagged(own_maps, carried, pixmask, lag_count) * inverse_area
        )
        return (carried, tables, stored)

    _, tables, stored = lax.fori_loop(1, bin_count, advance, (own_maps, initial, stored_init))
    pair_table = lax.psum(tables, ("bin", "sky"))
    left_hot = (bin_pairs[:, 0:1] == indices[None, :]).astype(jnp.float32)
    right_hot = (bin_pairs[:, 1:2] == indices[None, :]).astype(jnp.float32)
    corr_table = jnp.einsum("pi,pj,ijsl->psl", left_hot, right_hot, pair_table, precision=HIGH)
    pair_grad = pair_weight * (corr_table - target_corr)
    table_grad = jnp.einsum("pi,pj,psl->ijsl", left_hot, right_hot, pair_grad, precision=HIGH)
    own_block = take_block(table_grad, mine_hot, mine_hot)
    start_grad = adjoint_lags(own_maps, own_block, own_block, pixmask)

    def partner_term(visitor, k):
        other_hot = bin_hot(k)
        return adjoint_lags(
            visitor,
            take_block(table_grad, mine_hot, other_hot),
            take_block(table_grad, other_hot, mine_hot),
            pixmask,
        )

    def reread(k, totals):
        visitor = lax.dynamic_index_in_dim(stored, k - 1, 0, keepdims=False)
        return totals + partner_term(visitor, k)

    totals = lax.fori_loop(1, visit_count + 1, reread, start_grad)
    col_pass = adjoint_cols(totals, filter_taps)
    widened = with_halo(col_pass, (("sky", 1),), half_width)
    map_grad = adjoint_rows(widened, filter_taps, row_count)
    return (corr_table, map_grad[None])


def solution(mesh):
    placed = (P("bin", "sky", None), P(), P("sky", None), P(), P(), P())
    return jax.shard_map(
        per_device,
        mesh=mesh,
        in_specs=placed,
        out_specs=(P(), P("bin", "sky", None)),
        check_vma=False,
    )
```

profile of v0, /device:TPU:9, one launch (start us, length us, event | category | flops | bytes accessed | tf_op | source)
XLA Modules:
  0.0 306.5 jit_solution(4904538330784414321)
XLA Ops:
  0.6 3.7 %collective-permute-start.1 = (bf16[8,8192]{1,0:T(8,128)(2,1)}, bf16[8,8192]{1,0:T(8,128)(2,1)S(1)}, u32[]{:S(2)}, u32[]{:S(2)}) collective-permute-start(bf16[8,8192]{1,0:T(8,128)(2,1)} %bitcast.118), channel_id=1, source_target_pairs={{0,1},{1,2},{2,3},{4,5},{5,6},{6,7},{8,9},{9,10},{10,11},{12,13},{... | collective-permute-start | bytes 393224 | tf_op jit(solution)/shard_map/ppermute | solution.py:14
  4.3 1.9 collective-permute-start.2
  8.1 1.8 slice_reduce_fusion.16
  10.8 1.0 maximum_convert_fusion
  12.1 1.8 multiply_add_fusion.4
  14.0 5.9 %fusion.112 = (f32[5,8,8192]{2,1,0:T(8,128)S(1)}, bf16[5,8,8192]{2,1,0:T(8,128)(2,1)S(1)}) fusion(f32[5]{0:T(128)S(1)} %get-tuple-element.778, f32[5]{0:T(128)S(1)} %get-tuple-element.779, f32[5]{0:T(128)S(1)} %get-tuple-element.764, f32[5]{0:T(128)S(1)} %get-tuple-element.765, f32[5]{0:T(128)S(1)} %get-tuple-element.766, f32[5]{0:T(128)S(1)} %get-tuple-element.767, ...), kind=kLoop, calls=%fused_computation.223 | loop fusion | flops 11468800 | bytes 3277140 | tf_op jit(solution)/shard_map/convert_element_type | solution.py:57
  20.8 1.7 slice_multiply_fusion.11
  22.5 2.1 slice_multiply_fusion.9
  24.6 2.1 slice_multiply_fusion.7
  27.2 143.4 %while.42 = (s32[]{:T(128)}, bf16[5,8,8192]{2,1,0:T(8,128)(2,1)}, f32[8,8,5,4]{1,3,2,0:T(4,128)S(1)}, bf16[7,5,8,8192]{3,2,1,0:T(8,128)(2,1)}, s32[]{:T(128)}, /...) while((s32[]{:T(128)}, bf16[5,8,8192]{2,1,0:T(8,128)(2,1)}, ...), condition=%wide.region_9.10_spmd.clone.clone, body=%wide.region_4.9_spmd.clone.clone.sunk | while | flops 6555130 | bytes 10627522 | solution.py:156
  27.2 1.3 collective-permute-start
  28.6 14.0 %collective-permute-done = bf16[5,8,8192]{2,1,0:T(8,128)(2,1)S(1)} collective-permute-done((bf16[5,8,8192]{2,1,0:T(8,128)(2,1)}, bf16[5,8,8192]{2,1,0:T(8,128)(2,1)S(1)}, u32[]{:S(2)}, u32[]{:S(2)}) %collective-permute-start) | collective-permute-done | bytes 655392 | tf_op jit(solution)/shard_map/while/body/eval_jaxpr/ppermute | solution.py:25
  46.6 16.1 %collective-permute-done = bf16[5,8,8192]{2,1,0:T(8,128)(2,1)S(1)} collective-permute-done((bf16[5,8,8192]{2,1,0:T(8,128)(2,1)}, bf16[5,8,8192]{2,1,0:T(8,128)(2,1)S(1)}, u32[]{:S(2)}, u32[]{:S(2)}) %collective-permute-start) | collective-permute-done | bytes 655392 | tf_op jit(solution)/shard_map/while/body/eval_jaxpr/ppermute | solution.py:25
  66.4 17.7 %collective-permute-done = bf16[5,8,8192]{2,1,0:T(8,128)(2,1)S(1)} collective-permute-done((bf16[5,8,8192]{2,1,0:T(8,128)(2,1)}, bf16[5,8,8192]{2,1,0:T(8,128)(2,1)S(1)}, u32[]{:S(2)}, u32[]{:S(2)}) %collective-permute-start) | collective-permute-done | bytes 655392 | tf_op jit(solution)/shard_map/while/body/eval_jaxpr/ppermute | solution.py:25
  87.8 16.9 %collective-permute-done = bf16[5,8,8192]{2,1,0:T(8,128)(2,1)S(1)} collective-permute-done((bf16[5,8,8192]{2,1,0:T(8,128)(2,1)}, bf16[5,8,8192]{2,1,0:T(8,128)(2,1)S(1)}, u32[]{:S(2)}, u32[]{:S(2)}) %collective-permute-start) | collective-permute-done | bytes 655392 | tf_op jit(solution)/shard_map/while/body/eval_jaxpr/ppermute | solution.py:25
  108.4 18.1 %collective-permute-done = bf16[5,8,8192]{2,1,0:T(8,128)(2,1)S(1)} collective-permute-done((bf16[5,8,8192]{2,1,0:T(8,128)(2,1)}, bf16[5,8,8192]{2,1,0:T(8,128)(2,1)S(1)}, u32[]{:S(2)}, u32[]{:S(2)}) %collective-permute-start) | collective-permute-done | bytes 655392 | tf_op jit(solution)/shard_map/while/body/eval_jaxpr/ppermute | solution.py:25
  130.2 17.0 %collective-permute-done = bf16[5,8,8192]{2,1,0:T(8,128)(2,1)S(1)} collective-permute-done((bf16[5,8,8192]{2,1,0:T(8,128)(2,1)}, bf16[5,8,8192]{2,1,0:T(8,128)(2,1)S(1)}, u32[]{:S(2)}, u32[]{:S(2)}) %collective-permute-start) | collective-permute-done | bytes 655392 | tf_op jit(solution)/shard_map/while/body/eval_jaxpr/ppermute | solution.py:25
  150.9 16.2 %collective-permute-done = bf16[5,8,8192]{2,1,0:T(8,128)(2,1)S(1)} collective-permute-done((bf16[5,8,8192]{2,1,0:T(8,128)(2,1)}, bf16[5,8,8192]{2,1,0:T(8,128)(2,1)S(1)}, u32[]{:S(2)}, u32[]{:S(2)}) %collective-permute-start) | collective-permute-done | bytes 655392 | tf_op jit(solution)/shard_map/while/body/eval_jaxpr/ppermute | solution.py:25
  170.7 47.8 %psum.7 = f32[8,8,5,4]{1,2,0,3:T(8,128)S(1)} all-reduce(f32[8,8,5,4]{1,2,0,3:T(8,128)S(1)} %copy.10), channel_id=1, replica_groups=mesh['bin'=8,'sky'=4] {'bin','sky'}, use_global_device_ids=true, to_apply=%region_10.11 | all-reduce | flops 1280 | bytes 10240 | tf_op jit(solution)/shard_map/psum | solution.py:157
  219.9 4.0 %fusion.78 = f32[5,8,8192]{2,1,0:T(8,128)S(1)} fusion(f32[5,8,8189]{2,1,0:T(8,128)} %get-tuple-element.843, f32[5,8,8189]{2,1,0:T(8,128)} %get-tuple-element.842, f32[5,8,8190]{2,1,0:T(8,128)} %get-tuple-element.841, f32[5,8,8190]{2,1,0:T(8,128)} %get-tuple-element.840, f32[5,8,8191]{2,1,0:T(8,128)} %get-tuple-element.839, ...), kind=kLoop, calls=%fused_computation.126 | loop fusion | flops 4915200 | bytes 9861328 | tf_op jit(solution)/shard_map/add | solution.py:76
  224.0 47.2 %while.43 = (s32[]{:T(128)}, f32[5,8,8192]{2,1,0:T(8,128)S(1)}, s32[]{:T(128)}, f32[8,8,5,4]{1,3,2,0:T(4,128)S(1)}, bf16[7,5,8,8192]{3,2,1,0:T(8,128)(2,1)}, /*i...) while((s32[]{:T(128)}, f32[5,8,8192]{2,1,0:T(8,128)S(1)}, ...), condition=%wide.region_12.13_spmd.clone.clone, body=%wide.region_11.12_spmd.clone.clone.sunk | while | flops 7554175 | bytes 28974256 | solution.py:179
  224.4 1.0 convolution_bitcast_fusion.4
  225.8 1.2 bitcast_convert_fusion.2
  228.3 2.4 fusion.128
  231.2 1.0 convolution_bitcast_fusion.4
  232.6 1.2 bitcast_convert_fusion.2
  235.0 2.4 fusion.128
  237.9 1.0 convolution_bitcast_fusion.4
  239.3 1.2 bitcast_convert_fusion.2
  241.8 2.4 fusion.128
  244.6 1.0 convolution_bitcast_fusion.4
  246.1 1.2 bitcast_convert_fusion.2
  248.5 2.4 fusion.128
  251.4 1.0 convolution_bitcast_fusion.4
  252.8 1.2 bitcast_convert_fusion.2
  255.3 2.4 fusion.128
  258.1 1.0 convolution_bitcast_fusion.4
  259.5 1.2 bitcast_convert_fusion.2
  262.0 2.4 fusion.128
  264.9 1.0 convolution_bitcast_fusion.4
  266.3 1.2 bitcast_convert_fusion.2
  268.7 2.4 fusion.128
  271.2 5.9 %multiply_add_fusion.3 = f32[5,8,8192]{2,1,0:T(8,128)S(1)} fusion(f32[5,8,8192]{2,1,0:T(8,128)S(1)} %get-tuple-element.629, f32[5]{0:T(128)S(1)} %copy-done.9, f32[5]{0:T(128)S(1)} %copy-done.11, f32[5]{0:T(128)S(1)} %get-tuple-element.764, f32[5]{0:T(128)S(1)} %get-tuple-element.765, f32[5]{0:T(128)S(1)} %get-tuple-element.766, ...), kind=kLoop, calls=%fused_computation.127 | loop fusion | flops 10813440 | bytes 2621780 | tf_op jit(solution)/shard_map/add | solution.py:89
  277.1 5.3 %collective-permute-start.3 = (f32[5,8,8192]{2,1,0:T(8,128)S(1)}, f32[5,8,8192]{2,1,0:T(8,128)S(1)}, u32[]{:S(2)}, u32[]{:S(2)}) collective-permute-start(f32[5,8,8192]{2,1,0:T(8,128)S(1)} %multiply_add_fusion.3), channel_id=1, source_target_pairs={{0,1},{1,2},{2,3},{4,5},{5,6},{6,7},{8,9},{9,10},{10,11},{12,13},{... | collective-permute-start | bytes 3932168 | tf_op jit(solution)/shard_map/ppermute | solution.py:14
  282.4 1.9 collective-permute-start.4
  284.9 12.0 %collective-permute-done.3 = f32[5,8,8192]{2,1,0:T(8,128)S(1)} collective-permute-done((f32[5,8,8192]{2,1,0:T(8,128)S(1)}, f32[5,8,8192]{2,1,0:T(8,128)S(1)}, u32[]{:S(2)}, u32[]{:S(2)}) %collective-permute-start.3) | collective-permute-done | bytes 1310752 | tf_op jit(solution)/shard_map/ppermute | solution.py:14
  296.9 4.4 %collective-permute-done.4 = f32[5,8,8192]{2,1,0:T(8,128)S(1)} collective-permute-done((f32[5,8,8192]{2,1,0:T(8,128)S(1)}, f32[5,8,8192]{2,1,0:T(8,128)S(1)}, u32[]{:S(2)}, u32[]{:S(2)}) %collective-permute-start.4) | collective-permute-done | bytes 1310752 | tf_op jit(solution)/shard_map/ppermute | solution.py:17
  301.3 5.2 %fusion.36 = f32[8,8192]{1,0:T(8,128)} fusion(f32[5,8,8192]{2,1,0:T(8,128)S(1)} %multiply_add_fusion.3, f32[5,8,8192]{2,1,0:T(8,128)S(1)} %collective-permute-done.4, f32[5,8,8192]{2,1,0:T(8,128)S(1)} %collective-permute-done.3, f32[5]{0:T(128)S(1)} %copy-done.9, f32[5]{0:T(128)S(1)} %copy-done.11, f32[5]{0:T(128)S(1)} %get-tuple-element.764, ...), kind=kLoop, calls=%fused_computation.75 | loop fusion | flops 15663104 | bytes 4194644 | tf_op jit(solution)/shard_map/reduce_sum | solution.py:101
  (239 shorter events, 46.9 us)
Async XLA Ops:
  0.6 9.4 %collective-permute-start.1 = (bf16[8,8192]{1,0:T(8,128)(2,1)}, bf16[8,8192]{1,0:T(8,128)(2,1)S(1)}, u32[]{:S(2)}, u32[]{:S(2)}) collective-permute-start(bf16[8,8192]{1,0:T(8,128)(2,1)} %bitcast.118), channel_id=1, source_target_pairs={{0,1},{1,2},{2,3},{4,5},{5,6},{6,7},{8,9},{9,10},{10,11},{12,13},{... | collective-permute-start | bytes 393224 | tf_op jit(solution)/shard_map/ppermute | solution.py:14
  4.3 6.5 %collective-permute-start.2 = (bf16[8,8192]{1,0:T(8,128)(2,1)}, bf16[8,8192]{1,0:T(8,128)(2,1)S(1)}, u32[]{:S(2)}, u32[]{:S(2)}) collective-permute-start(bf16[8,8192]{1,0:T(8,128)(2,1)} %bitcast.119), channel_id=1, source_target_pairs={{1,0},{2,1},{3,2},{5,4},{6,5},{7,6},{9,8},{10,9},{11,10},{13,12},{... | collective-permute-start | bytes 393224 | tf_op jit(solution)/shard_map/ppermute | solution.py:17
  9.9 4.0 %copy-start.2 = (f32[5]{0:T(128)}, f32[5]{0:T(128)S(1)}, u32[]{:S(2)}) copy-start(f32[5]{0:T(128)S(1)} %get-tuple-element.775) | copy-start | bytes 64
  9.9 4.0 %copy-start.4 = (f32[5]{0:T(128)}, f32[5]{0:T(128)S(1)}, u32[]{:S(2)}) copy-start(f32[5]{0:T(128)S(1)} %get-tuple-element.776) | copy-start | bytes 64
  10.0 4.0 %copy-start.6 = (f32[5]{0:T(128)}, f32[5]{0:T(128)S(1)}, u32[]{:S(2)}) copy-start(f32[5]{0:T(128)S(1)} %get-tuple-element.777) | copy-start | bytes 64
  10.0 4.0 %copy-start.8 = (f32[5]{0:T(128)}, f32[5]{0:T(128)S(1)}, u32[]{:S(2)}) copy-start(f32[5]{0:T(128)S(1)} %get-tuple-element.778) | copy-start | bytes 64
  10.0 4.0 %copy-start.10 = (f32[5]{0:T(128)}, f32[5]{0:T(128)S(1)}, u32[]{:S(2)}) copy-start(f32[5]{0:T(128)S(1)} %get-tuple-element.779) | copy-start | bytes 64
  27.2 191.7 %copy-start = (f32[36,5,4]{0,2,1:T(4,128)S(1)}, f32[36,5,4]{0,2,1:T(4,128)}, u32[]{:S(2)}) copy-start(f32[36,5,4]{0,2,1:T(4,128)} %param.15) | copy-start | bytes 8644
  27.2 191.7 %copy-start.1 = (f32[36,5,4]{0,2,1:T(4,128)S(1)}, f32[36,5,4]{0,2,1:T(4,128)}, u32[]{:S(2)}) copy-start(f32[36,5,4]{0,2,1:T(4,128)} %param.14) | copy-start | bytes 8644
  27.2 15.4 %collective-permute-start = (bf16[5,8,8192]{2,1,0:T(8,128)(2,1)}, bf16[5,8,8192]{2,1,0:T(8,128)(2,1)S(1)}, u32[]{:S(2)}, u32[]{:S(2)}) collective-permute-start(bf16[5,8,8192]{2,1,0:T(8,128)(2,1)} %get-tuple-element.1039), channel_id=1, source_target_pairs={{0,4},{4,8},{8,12},{12,16},{16,20},{20,24},{24,28},{28,0},{1,5},{5... | collective-permute-start | bytes 1966088 | tf_op jit(solution)/shard_map/while/body/eval_jaxpr/ppermute | solution.py:25
  46.2 16.5 %collective-permute-start = (bf16[5,8,8192]{2,1,0:T(8,128)(2,1)}, bf16[5,8,8192]{2,1,0:T(8,128)(2,1)S(1)}, u32[]{:S(2)}, u32[]{:S(2)}) collective-permute-start(bf16[5,8,8192]{2,1,0:T(8,128)(2,1)} %get-tuple-element.1039), channel_id=1, source_target_pairs={{0,4},{4,8},{8,12},{12,16},{16,20},{20,24},{24,28},{28,0},{1,5},{5... | collective-permute-start | bytes 1966088 | tf_op jit(solution)/shard_map/while/body/eval_jaxpr/ppermute | solution.py:25
  66.3 17.8 %collective-permute-start = (bf16[5,8,8192]{2,1,0:T(8,128)(2,1)}, bf16[5,8,8192]{2,1,0:T(8,128)(2,1)S(1)}, u32[]{:S(2)}, u32[]{:S(2)}) collective-permute-start(bf16[5,8,8192]{2,1,0:T(8,128)(2,1)} %get-tuple-element.1039), channel_id=1, source_target_pairs={{0,4},{4,8},{8,12},{12,16},{16,20},{20,24},{24,28},{28,0},{1,5},{5... | collective-permute-start | bytes 1966088 | tf_op jit(solution)/shard_map/while/body/eval_jaxpr/ppermute | solution.py:25
  87.7 17.0 %collective-permute-start = (bf16[5,8,8192]{2,1,0:T(8,128)(2,1)}, bf16[5,8,8192]{2,1,0:T(8,128)(2,1)S(1)}, u32[]{:S(2)}, u32[]{:S(2)}) collective-permute-start(bf16[5,8,8192]{2,1,0:T(8,128)(2,1)} %get-tuple-element.1039), channel_id=1, source_target_pairs={{0,4},{4,8},{8,12},{12,16},{16,20},{20,24},{24,28},{28,0},{1,5},{5... | collective-permute-start | bytes 1966088 | tf_op jit(solution)/shard_map/while/body/eval_jaxpr/ppermute | solution.py:25
  108.3 18.2 %collective-permute-start = (bf16[5,8,8192]{2,1,0:T(8,128)(2,1)}, bf16[5,8,8192]{2,1,0:T(8,128)(2,1)S(1)}, u32[]{:S(2)}, u32[]{:S(2)}) collective-permute-start(bf16[5,8,8192]{2,1,0:T(8,128)(2,1)} %get-tuple-element.1039), channel_id=1, source_target_pairs={{0,4},{4,8},{8,12},{12,16},{16,20},{20,24},{24,28},{28,0},{1,5},{5... | collective-permute-start | bytes 1966088 | tf_op jit(solution)/shard_map/while/body/eval_jaxpr/ppermute | solution.py:25
  130.1 17.1 %collective-permute-start = (bf16[5,8,8192]{2,1,0:T(8,128)(2,1)}, bf16[5,8,8192]{2,1,0:T(8,128)(2,1)S(1)}, u32[]{:S(2)}, u32[]{:S(2)}) collective-permute-start(bf16[5,8,8192]{2,1,0:T(8,128)(2,1)} %get-tuple-element.1039), channel_id=1, source_target_pairs={{0,4},{4,8},{8,12},{12,16},{16,20},{20,24},{24,28},{28,0},{1,5},{5... | collective-permute-start | bytes 1966088 | tf_op jit(solution)/shard_map/while/body/eval_jaxpr/ppermute | solution.py:25
  150.8 16.2 %collective-permute-start = (bf16[5,8,8192]{2,1,0:T(8,128)(2,1)}, bf16[5,8,8192]{2,1,0:T(8,128)(2,1)S(1)}, u32[]{:S(2)}, u32[]{:S(2)}) collective-permute-start(bf16[5,8,8192]{2,1,0:T(8,128)(2,1)} %get-tuple-element.1039), channel_id=1, source_target_pairs={{0,4},{4,8},{8,12},{12,16},{16,20},{20,24},{24,28},{28,0},{1,5},{5... | collective-permute-start | bytes 1966088 | tf_op jit(solution)/shard_map/while/body/eval_jaxpr/ppermute | solution.py:25
  223.9 47.2 %copy-start.3 = (f32[5]{0:T(128)S(1)}, f32[5]{0:T(128)}, u32[]{:S(2)}) copy-start(f32[5]{0:T(128)} %copy-done.2) | copy-start | bytes 64
  223.9 47.2 %copy-start.5 = (f32[5]{0:T(128)S(1)}, f32[5]{0:T(128)}, u32[]{:S(2)}) copy-start(f32[5]{0:T(128)} %copy-done.4) | copy-start | bytes 64
  223.9 47.2 %copy-start.7 = (f32[5]{0:T(128)S(1)}, f32[5]{0:T(128)}, u32[]{:S(2)}) copy-start(f32[5]{0:T(128)} %copy-done.6) | copy-start | bytes 64
  223.9 47.2 %copy-start.9 = (f32[5]{0:T(128)S(1)}, f32[5]{0:T(128)}, u32[]{:S(2)}) copy-start(f32[5]{0:T(128)} %copy-done.8) | copy-start | bytes 64
  224.0 47.2 %copy-start.11 = (f32[5]{0:T(128)S(1)}, f32[5]{0:T(128)}, u32[]{:S(2)}) copy-start(f32[5]{0:T(128)} %copy-done.10) | copy-start | bytes 64
  277.1 19.8 %collective-permute-start.3 = (f32[5,8,8192]{2,1,0:T(8,128)S(1)}, f32[5,8,8192]{2,1,0:T(8,128)S(1)}, u32[]{:S(2)}, u32[]{:S(2)}) collective-permute-start(f32[5,8,8192]{2,1,0:T(8,128)S(1)} %multiply_add_fusion.3), channel_id=1, source_target_pairs={{0,1},{1,2},{2,3},{4,5},{5,6},{6,7},{8,9},{9,10},{10,11},{12,13},{... | collective-permute-start | bytes 3932168 | tf_op jit(solution)/shard_map/ppermute | solution.py:14
  282.4 18.9 %collective-permute-start.4 = (f32[5,8,8192]{2,1,0:T(8,128)S(1)}, f32[5,8,8192]{2,1,0:T(8,128)S(1)}, u32[]{:S(2)}, u32[]{:S(2)}) collective-permute-start(f32[5,8,8192]{2,1,0:T(8,128)S(1)} %multiply_add_fusion.3), channel_id=1, source_target_pairs={{1,0},{2,1},{3,2},{5,4},{6,5},{7,6},{9,8},{10,9},{11,10},{13,12},{... | collective-permute-start | bytes 3932168 | tf_op jit(solution)/shard_map/ppermute | solution.py:17
where the time goes:
time: 307 us; the launch traced here: 306 us
  waiting for transfers between devices  133 us (43%)
  other arithmetic  79.3 us (26%)
  blocking collectives  47.8 us (16%)
  local copies, waits for them, and re-layouts  22 us (7%)
  starting transfers between devices  14.4 us (5%)
  matrix products  8.21 us (3%)
    ppermute x7, waiting for transfers between devices, shifted(): return lax.ppermute(value, axis, pairs)  116 us
    psum x1, blocking collectives, per_device(): pair_table = lax.psum(tables, ('bin', 'sky'))  47.8 us
    add x7, other arithmetic, reread(): return totals + partner_term(visitor, k)  16.7 us
    mul x24, other arithmetic, adjoint_lags(): joint_mask[None] * widened[:, :, offset:]  14.7 us
    ppermute x2, waiting for transfers between devices, with_halo(): lax.ppermute(lax.slice_in_dim(block, block.shape[dim] - width, None, axis...  12 us
    reduce_sum x29, other arithmetic, lagged(): columns.append(jnp.sum(product, axis=(1, 2)))  11.9 us
    while x42, local copies, waits for them, and re-layouts  8.95 us
    ppermute x2, starting transfers between devices, with_halo(): lax.ppermute(lax.slice_in_dim(block, block.shape[dim] - width, None, axis...  8.95 us
  transfers between devices with their start and end apart: 11, of which 10 were waited for; matrix products, arithmetic and copies ran while one was open for 2% of the time, Pallas kernels for 0%

commit v1 on v0

--- a/solution.py
+++ b/solution.py
@@ -154,7 +154,7 @@
         return (carried, tables, stored)
 
     _, tables, stored = lax.fori_loop(1, bin_count, advance, (own_maps, initial, stored_init))
-    pair_table = lax.psum(tables, ("bin", "sky"))
+    pair_table = lax.psum(lax.psum(tables, "sky"), "bin")
     left_hot = (bin_pairs[:, 0:1] == indices[None, :]).astype(jnp.float32)
     right_hot = (bin_pairs[:, 1:2] == indices[None, :]).astype(jnp.float32)
     corr_table = jnp.einsum("pi,pj,ijsl->psl", left_hot, right_hot, pair_table, precision=HIGH)

time: 307 us -> 312 us (1.016); the launches traced: 306 us -> 308 us
  starting transfers between devices: 14.4 us -> 18.6 us
    ppermute x2, starting transfers between devices: 8.95 us -> 13.1 us  [with_halo(): lax.ppermute(lax.slice_in_dim(block, block.shape[dim] - width, None, axis...]
    psum x1 -> x2, blocking collectives: 47.8 us -> 45 us  [per_device(): pair_table = lax.psum(lax.psum(tables, 'sky'), 'bin')]
where the time goes in v1:
time: 312 us; the launch traced here: 308 us
  waiting for transfers between devices  133 us (43%)
  other arithmetic  79.3 us (25%)
  blocking collectives  45 us (14%)
  local copies, waits for them, and re-layouts  22 us (7%)
  starting transfers between devices  18.6 us (6%)
  matrix products  8.21 us (3%)
    ppermute x7, waiting for transfers between devices, shifted(): return lax.ppermute(value, axis, pairs)  116 us
    psum x2, blocking collectives, per_device(): pair_table = lax.psum(lax.psum(tables, 'sky'), 'bin')  45 us
    add x7, other arithmetic, reread(): return totals + partner_term(visitor, k)  16.7 us
    mul x24, other arithmetic, adjoint_lags(): joint_mask[None] * widened[:, :, offset:]  14.7 us
    ppermute x2, starting transfers between devices, with_halo(): lax.ppermute(lax.slice_in_dim(block, block.shape[dim] - width, None, axis...  13.1 us
    ppermute x2, waiting for transfers between devices, with_halo(): lax.ppermute(lax.slice_in_dim(block, block.shape[dim] - width, None, axis...  12 us
    reduce_sum x29, other arithmetic, lagged(): columns.append(jnp.sum(product, axis=(1, 2)))  11.9 us
    while x42, local copies, waits for them, and re-layouts  8.95 us
  transfers between devices with their start and end apart: 11, of which 10 were waited for; matrix products, arithmetic and copies ran while one was open for 2% of the time, Pallas kernels for 0%

profile of v1, /device:TPU:9, one launch (start us, length us, event | category | flops | bytes accessed | tf_op | source)
XLA Modules:
  0.0 307.9 jit_solution(15167162142738725953)
XLA Ops:
  0.6 3.7 %collective-permute-start.1 = (bf16[8,8192]{1,0:T(8,128)(2,1)}, bf16[8,8192]{1,0:T(8,128)(2,1)S(1)}, u32[]{:S(2)}, u32[]{:S(2)}) collective-permute-start(bf16[8,8192]{1,0:T(8,128)(2,1)} %bitcast.118), channel_id=1, source_target_pairs={{0,1},{1,2},{2,3},{4,5},{5,6},{6,7},{8,9},{9,10},{10,11},{12,13},{... | collective-permute-start | bytes 393224 | tf_op jit(solution)/shard_map/ppermute | solution.py:14
  4.3 1.9 collective-permute-start.2
  8.1 1.8 slice_reduce_fusion.16
  12.1 1.8 multiply_add_fusion.4
  14.0 5.9 %fusion.112 = (f32[5,8,8192]{2,1,0:T(8,128)S(1)}, bf16[5,8,8192]{2,1,0:T(8,128)(2,1)S(1)}) fusion(f32[5]{0:T(128)S(1)} %get-tuple-element.778, f32[5]{0:T(128)S(1)} %get-tuple-element.779, f32[5]{0:T(128)S(1)} %get-tuple-element.764, f32[5]{0:T(128)S(1)} %get-tuple-element.765, f32[5]{0:T(128)S(1)} %get-tuple-element.766, f32[5]{0:T(128)S(1)} %get-tuple-element.767, ...), kind=kLoop, calls=%fused_computation.223 | loop fusion | flops 11468800 | bytes 3277140 | tf_op jit(solution)/shard_map/convert_element_type | solution.py:57
  20.8 1.7 slice_multiply_fusion.11
  22.5 2.1 slice_multiply_fusion.9
  24.6 2.1 slice_multiply_fusion.7
  27.2 143.4 %while.42 = (s32[]{:T(128)}, bf16[5,8,8192]{2,1,0:T(8,128)(2,1)}, f32[8,8,5,4]{1,3,2,0:T(4,128)S(1)}, bf16[7,5,8,8192]{3,2,1,0:T(8,128)(2,1)}, s32[]{:T(128)}, /...) while((s32[]{:T(128)}, bf16[5,8,8192]{2,1,0:T(8,128)(2,1)}, ...), condition=%wide.region_9.10_spmd.clone.clone, body=%wide.region_4.9_spmd.clone.clone.sunk | while | flops 6555130 | bytes 10627522 | solution.py:156
  27.2 1.3 collective-permute-start
  28.6 14.0 %collective-permute-done = bf16[5,8,8192]{2,1,0:T(8,128)(2,1)S(1)} collective-permute-done((bf16[5,8,8192]{2,1,0:T(8,128)(2,1)}, bf16[5,8,8192]{2,1,0:T(8,128)(2,1)S(1)}, u32[]{:S(2)}, u32[]{:S(2)}) %collective-permute-start) | collective-permute-done | bytes 655392 | tf_op jit(solution)/shard_map/while/body/eval_jaxpr/ppermute | solution.py:25
  46.6 16.1 %collective-permute-done = bf16[5,8,8192]{2,1,0:T(8,128)(2,1)S(1)} collective-permute-done((bf16[5,8,8192]{2,1,0:T(8,128)(2,1)}, bf16[5,8,8192]{2,1,0:T(8,128)(2,1)S(1)}, u32[]{:S(2)}, u32[]{:S(2)}) %collective-permute-start) | collective-permute-done | bytes 655392 | tf_op jit(solution)/shard_map/while/body/eval_jaxpr/ppermute | solution.py:25
  66.4 17.7 %collective-permute-done = bf16[5,8,8192]{2,1,0:T(8,128)(2,1)S(1)} collective-permute-done((bf16[5,8,8192]{2,1,0:T(8,128)(2,1)}, bf16[5,8,8192]{2,1,0:T(8,128)(2,1)S(1)}, u32[]{:S(2)}, u32[]{:S(2)}) %collective-permute-start) | collective-permute-done | bytes 655392 | tf_op jit(solution)/shard_map/while/body/eval_jaxpr/ppermute | solution.py:25
  87.8 16.9 %collective-permute-done = bf16[5,8,8192]{2,1,0:T(8,128)(2,1)S(1)} collective-permute-done((bf16[5,8,8192]{2,1,0:T(8,128)(2,1)}, bf16[5,8,8192]{2,1,0:T(8,128)(2,1)S(1)}, u32[]{:S(2)}, u32[]{:S(2)}) %collective-permute-start) | collective-permute-done | bytes 655392 | tf_op jit(solution)/shard_map/while/body/eval_jaxpr/ppermute | solution.py:25
  108.4 18.1 %collective-permute-done = bf16[5,8,8192]{2,1,0:T(8,128)(2,1)S(1)} collective-permute-done((bf16[5,8,8192]{2,1,0:T(8,128)(2,1)}, bf16[5,8,8192]{2,1,0:T(8,128)(2,1)S(1)}, u32[]{:S(2)}, u32[]{:S(2)}) %collective-permute-start) | collective-permute-done | bytes 655392 | tf_op jit(solution)/shard_map/while/body/eval_jaxpr/ppermute | solution.py:25
  130.2 17.0 %collective-permute-done = bf16[5,8,8192]{2,1,0:T(8,128)(2,1)S(1)} collective-permute-done((bf16[5,8,8192]{2,1,0:T(8,128)(2,1)}, bf16[5,8,8192]{2,1,0:T(8,128)(2,1)S(1)}, u32[]{:S(2)}, u32[]{:S(2)}) %collective-permute-start) | collective-permute-done | bytes 655392 | tf_op jit(solution)/shard_map/while/body/eval_jaxpr/ppermute | solution.py:25
  150.9 16.2 %collective-permute-done = bf16[5,8,8192]{2,1,0:T(8,128)(2,1)S(1)} collective-permute-done((bf16[5,8,8192]{2,1,0:T(8,128)(2,1)}, bf16[5,8,8192]{2,1,0:T(8,128)(2,1)S(1)}, u32[]{:S(2)}, u32[]{:S(2)}) %collective-permute-start) | collective-permute-done | bytes 655392 | tf_op jit(solution)/shard_map/while/body/eval_jaxpr/ppermute | solution.py:25
  170.7 13.8 %psum.14 = f32[8,8,5,4]{1,2,0,3:T(8,128)S(1)} all-reduce(f32[8,8,5,4]{1,2,0,3:T(8,128)S(1)} %copy.10), channel_id=1, replica_groups=mesh['bin'=8,'sky'=4] {'sky'}, use_global_device_ids=true, to_apply=%region_10.11 | all-reduce | flops 1280 | bytes 10240 | tf_op jit(solution)/shard_map/psum | solution.py:157
  184.4 31.2 %psum.15 = f32[8,8,5,4]{1,2,0,3:T(8,128)S(1)} all-reduce(f32[8,8,5,4]{1,2,0,3:T(8,128)S(1)} %psum.14), channel_id=1, replica_groups=mesh['bin'=8,'sky'=4] {'bin'}, use_global_device_ids=true, to_apply=%region_11.12 | all-reduce | flops 1280 | bytes 10240 | tf_op jit(solution)/shard_map/psum | solution.py:157
  217.1 4.0 %fusion.78 = f32[5,8,8192]{2,1,0:T(8,128)S(1)} fusion(f32[5,8,8189]{2,1,0:T(8,128)} %get-tuple-element.843, f32[5,8,8189]{2,1,0:T(8,128)} %get-tuple-element.842, f32[5,8,8190]{2,1,0:T(8,128)} %get-tuple-element.841, f32[5,8,8190]{2,1,0:T(8,128)} %get-tuple-element.840, f32[5,8,8191]{2,1,0:T(8,128)} %get-tuple-element.839, ...), kind=kLoop, calls=%fused_computation.126 | loop fusion | flops 4915200 | bytes 9861328 | tf_op jit(solution)/shard_map/add | solution.py:76
  221.2 47.2 %while.43 = (s32[]{:T(128)}, f32[5,8,8192]{2,1,0:T(8,128)S(1)}, s32[]{:T(128)}, f32[8,8,5,4]{1,3,2,0:T(4,128)S(1)}, bf16[7,5,8,8192]{3,2,1,0:T(8,128)(2,1)}, /*i...) while((s32[]{:T(128)}, f32[5,8,8192]{2,1,0:T(8,128)S(1)}, ...), condition=%wide.region_13.14_spmd.clone.clone, body=%wide.region_12.13_spmd.clone.clone.sunk | while | flops 7554175 | bytes 28974256 | solution.py:179
  221.7 1.0 convolution_bitcast_fusion.4
  223.1 1.2 bitcast_convert_fusion.2
  225.5 2.4 fusion.128
  228.4 1.0 convolution_bitcast_fusion.4
  229.8 1.2 bitcast_convert_fusion.2
  232.3 2.4 fusion.128
  235.1 1.0 convolution_bitcast_fusion.4
  236.5 1.2 bitcast_convert_fusion.2
  239.0 2.4 fusion.128
  241.9 1.0 convolution_bitcast_fusion.4
  243.3 1.2 bitcast_convert_fusion.2
  245.7 2.4 fusion.128
  248.6 1.0 convolution_bitcast_fusion.4
  250.0 1.2 bitcast_convert_fusion.2
  252.5 2.4 fusion.128
  255.3 1.0 convolution_bitcast_fusion.4
  256.8 1.2 bitcast_convert_fusion.2
  259.2 2.4 fusion.128
  262.1 1.0 convolution_bitcast_fusion.4
  263.5 1.2 bitcast_convert_fusion.2
  266.0 2.4 fusion.128
  268.4 5.9 %multiply_add_fusion.3 = f32[5,8,8192]{2,1,0:T(8,128)S(1)} fusion(f32[5,8,8192]{2,1,0:T(8,128)S(1)} %get-tuple-element.629, f32[5]{0:T(128)S(1)} %copy-done.9, f32[5]{0:T(128)S(1)} %copy-done.11, f32[5]{0:T(128)S(1)} %get-tuple-element.764, f32[5]{0:T(128)S(1)} %get-tuple-element.765, f32[5]{0:T(128)S(1)} %get-tuple-element.766, ...), kind=kLoop, calls=%fused_computation.127 | loop fusion | flops 10813440 | bytes 2621780 | tf_op jit(solution)/shard_map/add | solution.py:89
  274.4 9.5 %collective-permute-start.3 = (f32[5,8,8192]{2,1,0:T(8,128)S(1)}, f32[5,8,8192]{2,1,0:T(8,128)S(1)}, u32[]{:S(2)}, u32[]{:S(2)}) collective-permute-start(f32[5,8,8192]{2,1,0:T(8,128)S(1)} %multiply_add_fusion.3), channel_id=1, source_target_pairs={{0,1},{1,2},{2,3},{4,5},{5,6},{6,7},{8,9},{9,10},{10,11},{12,13},{... | collective-permute-start | bytes 3932168 | tf_op jit(solution)/shard_map/ppermute | solution.py:14
  283.8 1.9 collective-permute-start.4
  286.4 12.0 %collective-permute-done.3 = f32[5,8,8192]{2,1,0:T(8,128)S(1)} collective-permute-done((f32[5,8,8192]{2,1,0:T(8,128)S(1)}, f32[5,8,8192]{2,1,0:T(8,128)S(1)}, u32[]{:S(2)}, u32[]{:S(2)}) %collective-permute-start.3) | collective-permute-done | bytes 1310752 | tf_op jit(solution)/shard_map/ppermute | solution.py:14
  298.4 4.4 %collective-permute-done.4 = f32[5,8,8192]{2,1,0:T(8,128)S(1)} collective-permute-done((f32[5,8,8192]{2,1,0:T(8,128)S(1)}, f32[5,8,8192]{2,1,0:T(8,128)S(1)}, u32[]{:S(2)}, u32[]{:S(2)}) %collective-permute-start.4) | collective-permute-done | bytes 1310752 | tf_op jit(solution)/shard_map/ppermute | solution.py:17
  302.7 5.2 %fusion.36 = f32[8,8192]{1,0:T(8,128)} fusion(f32[5,8,8192]{2,1,0:T(8,128)S(1)} %multiply_add_fusion.3, f32[5,8,8192]{2,1,0:T(8,128)S(1)} %collective-permute-done.4, f32[5,8,8192]{2,1,0:T(8,128)S(1)} %collective-permute-done.3, f32[5]{0:T(128)S(1)} %copy-done.9, f32[5]{0:T(128)S(1)} %copy-done.11, f32[5]{0:T(128)S(1)} %get-tuple-element.764, ...), kind=kLoop, calls=%fused_computation.75 | loop fusion | flops 15663104 | bytes 4194644 | tf_op jit(solution)/shard_map/reduce_sum | solution.py:101
  (240 shorter events, 47.8 us)
Async XLA Ops:
  0.6 9.4 %collective-permute-start.1 = (bf16[8,8192]{1,0:T(8,128)(2,1)}, bf16[8,8192]{1,0:T(8,128)(2,1)S(1)}, u32[]{:S(2)}, u32[]{:S(2)}) collective-permute-start(bf16[8,8192]{1,0:T(8,128)(2,1)} %bitcast.118), channel_id=1, source_target_pairs={{0,1},{1,2},{2,3},{4,5},{5,6},{6,7},{8,9},{9,10},{10,11},{12,13},{... | collective-permute-start | bytes 393224 | tf_op jit(solution)/shard_map/ppermute | solution.py:14
  4.3 6.5 %collective-permute-start.2 = (bf16[8,8192]{1,0:T(8,128)(2,1)}, bf16[8,8192]{1,0:T(8,128)(2,1)S(1)}, u32[]{:S(2)}, u32[]{:S(2)}) collective-permute-start(bf16[8,8192]{1,0:T(8,128)(2,1)} %bitcast.119), channel_id=1, source_target_pairs={{1,0},{2,1},{3,2},{5,4},{6,5},{7,6},{9,8},{10,9},{11,10},{13,12},{... | collective-permute-start | bytes 393224 | tf_op jit(solution)/shard_map/ppermute | solution.py:17
  9.9 4.0 %copy-start.2 = (f32[5]{0:T(128)}, f32[5]{0:T(128)S(1)}, u32[]{:S(2)}) copy-start(f32[5]{0:T(128)S(1)} %get-tuple-element.775) | copy-start | bytes 64
  9.9 4.0 %copy-start.4 = (f32[5]{0:T(128)}, f32[5]{0:T(128)S(1)}, u32[]{:S(2)}) copy-start(f32[5]{0:T(128)S(1)} %get-tuple-element.776) | copy-start | bytes 64
  10.0 4.0 %copy-start.6 = (f32[5]{0:T(128)}, f32[5]{0:T(128)S(1)}, u32[]{:S(2)}) copy-start(f32[5]{0:T(128)S(1)} %get-tuple-element.777) | copy-start | bytes 64
  10.0 4.0 %copy-start.8 = (f32[5]{0:T(128)}, f32[5]{0:T(128)S(1)}, u32[]{:S(2)}) copy-start(f32[5]{0:T(128)S(1)} %get-tuple-element.778) | copy-start | bytes 64
  10.0 4.0 %copy-start.10 = (f32[5]{0:T(128)}, f32[5]{0:T(128)S(1)}, u32[]{:S(2)}) copy-start(f32[5]{0:T(128)S(1)} %get-tuple-element.779) | copy-start | bytes 64
  27.2 188.9 %copy-start = (f32[36,5,4]{0,2,1:T(4,128)S(1)}, f32[36,5,4]{0,2,1:T(4,128)}, u32[]{:S(2)}) copy-start(f32[36,5,4]{0,2,1:T(4,128)} %param.15) | copy-start | bytes 8644
  27.2 188.9 %copy-start.1 = (f32[36,5,4]{0,2,1:T(4,128)S(1)}, f32[36,5,4]{0,2,1:T(4,128)}, u32[]{:S(2)}) copy-start(f32[36,5,4]{0,2,1:T(4,128)} %param.14) | copy-start | bytes 8644
  27.2 15.4 %collective-permute-start = (bf16[5,8,8192]{2,1,0:T(8,128)(2,1)}, bf16[5,8,8192]{2,1,0:T(8,128)(2,1)S(1)}, u32[]{:S(2)}, u32[]{:S(2)}) collective-permute-start(bf16[5,8,8192]{2,1,0:T(8,128)(2,1)} %get-tuple-element.1039), channel_id=1, source_target_pairs={{0,4},{4,8},{8,12},{12,16},{16,20},{20,24},{24,28},{28,0},{1,5},{5... | collective-permute-start | bytes 1966088 | tf_op jit(solution)/shard_map/while/body/eval_jaxpr/ppermute | solution.py:25
  46.2 16.5 %collective-permute-start = (bf16[5,8,8192]{2,1,0:T(8,128)(2,1)}, bf16[5,8,8192]{2,1,0:T(8,128)(2,1)S(1)}, u32[]{:S(2)}, u32[]{:S(2)}) collective-permute-start(bf16[5,8,8192]{2,1,0:T(8,128)(2,1)} %get-tuple-element.1039), channel_id=1, source_target_pairs={{0,4},{4,8},{8,12},{12,16},{16,20},{20,24},{24,28},{28,0},{1,5},{5... | collective-permute-start | bytes 1966088 | tf_op jit(solution)/shard_map/while/body/eval_jaxpr/ppermute | solution.py:25
  66.3 17.8 %collective-permute-start = (bf16[5,8,8192]{2,1,0:T(8,128)(2,1)}, bf16[5,8,8192]{2,1,0:T(8,128)(2,1)S(1)}, u32[]{:S(2)}, u32[]{:S(2)}) collective-permute-start(bf16[5,8,8192]{2,1,0:T(8,128)(2,1)} %get-tuple-element.1039), channel_id=1, source_target_pairs={{0,4},{4,8},{8,12},{12,16},{16,20},{20,24},{24,28},{28,0},{1,5},{5... | collective-permute-start | bytes 1966088 | tf_op jit(solution)/shard_map/while/body/eval_jaxpr/ppermute | solution.py:25
  87.7 17.0 %collective-permute-start = (bf16[5,8,8192]{2,1,0:T(8,128)(2,1)}, bf16[5,8,8192]{2,1,0:T(8,128)(2,1)S(1)}, u32[]{:S(2)}, u32[]{:S(2)}) collective-permute-start(bf16[5,8,8192]{2,1,0:T(8,128)(2,1)} %get-tuple-element.1039), channel_id=1, source_target_pairs={{0,4},{4,8},{8,12},{12,16},{16,20},{20,24},{24,28},{28,0},{1,5},{5... | collective-permute-start | bytes 1966088 | tf_op jit(solution)/shard_map/while/body/eval_jaxpr/ppermute | solution.py:25
  108.3 18.2 %collective-permute-start = (bf16[5,8,8192]{2,1,0:T(8,128)(2,1)}, bf16[5,8,8192]{2,1,0:T(8,128)(2,1)S(1)}, u32[]{:S(2)}, u32[]{:S(2)}) collective-permute-start(bf16[5,8,8192]{2,1,0:T(8,128)(2,1)} %get-tuple-element.1039), channel_id=1, source_target_pairs={{0,4},{4,8},{8,12},{12,16},{16,20},{20,24},{24,28},{28,0},{1,5},{5... | collective-permute-start | bytes 1966088 | tf_op jit(solution)/shard_map/while/body/eval_jaxpr/ppermute | solution.py:25
  130.1 17.1 %collective-permute-start = (bf16[5,8,8192]{2,1,0:T(8,128)(2,1)}, bf16[5,8,8192]{2,1,0:T(8,128)(2,1)S(1)}, u32[]{:S(2)}, u32[]{:S(2)}) collective-permute-start(bf16[5,8,8192]{2,1,0:T(8,128)(2,1)} %get-tuple-element.1039), channel_id=1, source_target_pairs={{0,4},{4,8},{8,12},{12,16},{16,20},{20,24},{24,28},{28,0},{1,5},{5... | collective-permute-start | bytes 1966088 | tf_op jit(solution)/shard_map/while/body/eval_jaxpr/ppermute | solution.py:25
  150.8 16.2 %collective-permute-start = (bf16[5,8,8192]{2,1,0:T(8,128)(2,1)}, bf16[5,8,8192]{2,1,0:T(8,128)(2,1)S(1)}, u32[]{:S(2)}, u32[]{:S(2)}) collective-permute-start(bf16[5,8,8192]{2,1,0:T(8,128)(2,1)} %get-tuple-element.1039), channel_id=1, source_target_pairs={{0,4},{4,8},{8,12},{12,16},{16,20},{20,24},{24,28},{28,0},{1,5},{5... | collective-permute-start | bytes 1966088 | tf_op jit(solution)/shard_map/while/body/eval_jaxpr/ppermute | solution.py:25
  221.1 47.2 %copy-start.3 = (f32[5]{0:T(128)S(1)}, f32[5]{0:T(128)}, u32[]{:S(2)}) copy-start(f32[5]{0:T(128)} %copy-done.2) | copy-start | bytes 64
  221.1 47.2 %copy-start.5 = (f32[5]{0:T(128)S(1)}, f32[5]{0:T(128)}, u32[]{:S(2)}) copy-start(f32[5]{0:T(128)} %copy-done.4) | copy-start | bytes 64
  221.2 47.2 %copy-start.7 = (f32[5]{0:T(128)S(1)}, f32[5]{0:T(128)}, u32[]{:S(2)}) copy-start(f32[5]{0:T(128)} %copy-done.6) | copy-start | bytes 64
  221.2 47.2 %copy-start.9 = (f32[5]{0:T(128)S(1)}, f32[5]{0:T(128)}, u32[]{:S(2)}) copy-start(f32[5]{0:T(128)} %copy-done.8) | copy-start | bytes 64
  221.2 47.2 %copy-start.11 = (f32[5]{0:T(128)S(1)}, f32[5]{0:T(128)}, u32[]{:S(2)}) copy-start(f32[5]{0:T(128)} %copy-done.10) | copy-start | bytes 64
  274.4 24.0 %collective-permute-start.3 = (f32[5,8,8192]{2,1,0:T(8,128)S(1)}, f32[5,8,8192]{2,1,0:T(8,128)S(1)}, u32[]{:S(2)}, u32[]{:S(2)}) collective-permute-start(f32[5,8,8192]{2,1,0:T(8,128)S(1)} %multiply_add_fusion.3), channel_id=1, source_target_pairs={{0,1},{1,2},{2,3},{4,5},{5,6},{6,7},{8,9},{9,10},{10,11},{12,13},{... | collective-permute-start | bytes 3932168 | tf_op jit(solution)/shard_map/ppermute | solution.py:14
  283.8 18.9 %collective-permute-start.4 = (f32[5,8,8192]{2,1,0:T(8,128)S(1)}, f32[5,8,8192]{2,1,0:T(8,128)S(1)}, u32[]{:S(2)}, u32[]{:S(2)}) collective-permute-start(f32[5,8,8192]{2,1,0:T(8,128)S(1)} %multiply_add_fusion.3), channel_id=1, source_target_pairs={{1,0},{2,1},{3,2},{5,4},{6,5},{7,6},{9,8},{10,9},{11,10},{13,12},{... | collective-permute-start | bytes 3932168 | tf_op jit(solution)/shard_map/ppermute | solution.py:17
